TPU v7x, 32 devices: a whole 2x2x4 slice. The times are simulated.
32 devices in a mesh: branch: 2 (over y), res: 16 (over z, x, core).
Axes of the slice: x: 2, y: 2, z: 4, core: 2. Of those that a mesh axis runs over, the one named last changes fastest.
Arguments:
- alignment_representation: float32 [128, 96, 256], P(None, 'res'), may hold values from -6 to 6
- pairwise_state: float32 [96, 96, 128], P('res'), may hold values from -6 to 6
- alignment_mask: int32 [128, 96], P(None, 'res'), may hold values from 0 to 1, as said below
- residue_present_mask: int32 [96], P('res'), may hold values from 0 to 1, as said below
- row_projection_weight: float32 [4, 256, 256], replicated
- lateral_result_coeffs: float32 [256, 256], replicated, may hold values from -1.5 to 1.5
- pair_bias_weight: float32 [128, 8], replicated, may hold values from -0.75 to 0.75
- first_operand_coeffs: float32 [256, 32], replicated, may hold values from -0.375 to 0.375
- other_operand_coeffs: float32 [256, 32], replicated, may hold values from -0.375 to 0.375
- outer_output_weight: float32 [1024, 128], replicated, may hold values from -2 to 2
- starting_projection_weight: float32 [4, 128, 128], replicated
- starting_bias_weight: float32 [128, 4], replicated, may hold values from -0.75 to 0.75
- starting_output_weight: float32 [128, 128], replicated, may hold values from -2 to 2
- ending_projection_weight: float32 [4, 128, 128], replicated
- ending_bias_weight: float32 [128, 4], replicated, may hold values from -0.75 to 0.75
- ending_output_weight: float32 [128, 128], replicated, may hold values from -2 to 2
Outputs:
- alignment_output: float32 [128, 96, 256], P('branch', 'res')
- pairwise_output: float32 [96, 96, 128], P('res', None, 'branch')
Inputs may be any that keep to these rules, and one draw needn't show every extreme that they name: residue_present_mask is 1 on the first L residues and 0 on the rest, for a drawn L from 48 to 96. alignment_mask[s, r] is 1 exactly where s is below a drawn count from 32 to 128 and residue_present_mask[r] is 1.
All inputs are finite; a program needn't handle non-finite values.
Results may differ from a plain program's by a relative error of at most 0.0003.
Values sent between devices are 32-bit elements; how exact they have to be, the bound alone decides.
A program may use at most 128 MiB of HBM per device.

v0:
```python
import math
import jax
import jax.numpy as jnp
from jax import lax
from jax.sharding import PartitionSpec as P

ATTEND_HEADS = 8
HEADS_Z = 4
highest = lax.Precision.HIGHEST
epsilon = 1e-05
masked_score = -1000000000.0


def spread(value, axis, root):
    mine = lax.axis_index(axis) == root
    return lax.psum(jnp.where(mine, value, jnp.zeros_like(value)), axis)


def partner(block, axis, apart):
    count = lax.axis_size(axis)
    route = []
    for low in range(count):
        high = low | 1 << apart
        if high != low and high < count:
            route += [(low, high), (high, low)]
    return lax.ppermute(block, axis, route)


def layer_normalize(values):
    centred = values - jnp.mean(values, axis=-1, keepdims=True)
    variance = jnp.mean(centred * centred, axis=-1, keepdims=True)
    return centred * lax.rsqrt(variance + epsilon)


def linear_project(values, weight):
    return jnp.dot(values, weight, precision=highest, preferred_element_type=jnp.float32)


def attend(query_matrix, key_matrix, value_matrix, gate_matrix, score_bias, live_keys, head_count):
    head_width = query_matrix.shape[-1] // head_count
    shaped_q = query_matrix.reshape(query_matrix.shape[0], head_count, head_width)
    shaped_k = key_matrix.reshape(key_matrix.shape[0], head_count, head_width)
    shaped_v = value_matrix.reshape(value_matrix.shape[0], head_count, head_width)
    scores = (
        jnp.einsum("qhd,khd->hqk", shaped_q, shaped_k, precision=highest) / math.sqrt(head_width)
        + score_bias
    )
    scores = jnp.where(live_keys[None, None, :], scores, masked_score)
    scores = scores - jnp.max(scores, axis=-1, keepdims=True)
    weights = jnp.exp(scores)
    weights = weights / jnp.sum(weights, axis=-1, keepdims=True)
    mixture = jnp.einsum("hqk,khd->qhd", weights, shaped_v, precision=highest)
    return jax.nn.sigmoid(gate_matrix) * mixture.reshape(
        query_matrix.shape[0], head_count * head_width
    )


def factor_matrix(normed, float_mask, weight):
    return jnp.transpose(linear_project(normed, weight) * float_mask[:, :, None], (1, 2, 0))


def outer_block(left_matrix, mask_rows, right_all, mask_all, out_weight):
    residues, factor_width, sequences = right_all.shape

    def outer_one_row(operands):
        row_left, row_mask = operands
        outer_sum = jnp.einsum("cs,jes->jce", row_left, right_all, precision=highest)
        outer_sum = outer_sum.reshape(residues, factor_width * factor_width)
        intersection = jnp.einsum("ns,s->n", mask_all, row_mask, precision=highest)
        return linear_project(outer_sum, out_weight) / jnp.maximum(intersection, 1.0)[:, None]

    return lax.map(outer_one_row, (left_matrix, mask_rows))


def per_device(
    alignment_representation,
    pairwise_state,
    alignment_mask,
    residue_present_mask,
    row_projection_weight,
    lateral_result_coeffs,
    pair_bias_weight,
    first_operand_coeffs,
    other_operand_coeffs,
    outer_output_weight,
    starting_projection_weight,
    starting_bias_weight,
    starting_output_weight,
    ending_projection_weight,
    ending_bias_weight,
    ending_output_weight,
):
    alignment_present_flag = lax.axis_index("branch") == 0
    sequence_count = alignment_representation.shape[0]
    local_matrix = alignment_representation.shape[1]
    residues = pairwise_state.shape[1]
    pair_width = pairwise_state.shape[2]
    float_mask = alignment_mask.astype(jnp.float32)
    mask_rows = jnp.transpose(float_mask)
    update_dimensions = (local_matrix, residues, pair_width)

    def bias_rows_of(field):
        return jnp.einsum(
            "ijc,ch->hij", layer_normalize(field), pair_bias_weight, precision=highest
        )

    normed_alignment = layer_normalize(alignment_representation)
    handed = lax.cond(
        alignment_present_flag,
        lambda: jnp.zeros((pair_bias_weight.shape[1], local_matrix, residues), jnp.float32),
        lambda: bias_rows_of(pairwise_state),
    )
    own_rows = spread(handed, "branch", 1)
    row_bias = lax.all_gather(own_rows, "res", axis=1, tiled=True)
    seq_normed, seq_mask = (
        lax.all_to_all(normed_alignment, "res", split_axis=0, concat_axis=1, tiled=True),
        lax.all_to_all(float_mask, "res", split_axis=0, concat_axis=1, tiled=True),
    )

    def row_attention():
        query_matrix = linear_project(seq_normed, row_projection_weight[0])
        key_matrix = linear_project(seq_normed, row_projection_weight[1])
        value_matrix = linear_project(seq_normed, row_projection_weight[2])
        gate_matrix = linear_project(seq_normed, row_projection_weight[3])
        sequence_present = seq_mask > 0.5

        def one_sequence(operands):
            return attend(
                operands[0],
                operands[1],
                operands[2],
                operands[3],
                row_bias,
                operands[4],
                ATTEND_HEADS,
            )

        gated_output = lax.map(
            one_sequence, (query_matrix, key_matrix, value_matrix, gate_matrix, sequence_present)
        )
        return linear_project(gated_output, lateral_result_coeffs)

    row_change = lax.cond(alignment_present_flag, row_attention, lambda: jnp.zeros_like(seq_normed))
    alignment_delta = lax.all_to_all(row_change, "res", split_axis=1, concat_axis=0, tiled=True)
    alignment_result = alignment_representation + alignment_delta
    left_matrix = factor_matrix(normed_alignment, float_mask, first_operand_coeffs)
    right_matrix = factor_matrix(normed_alignment, float_mask, other_operand_coeffs)
    right_all, mask_all = (
        lax.all_gather(right_matrix, "res", axis=0, tiled=True),
        lax.all_gather(mask_rows, "res", axis=0, tiled=True),
    )
    update = lax.cond(
        alignment_present_flag,
        lambda: outer_block(left_matrix, mask_rows, right_all, mask_all, outer_output_weight),
        lambda: jnp.zeros(update_dimensions, jnp.float32),
    )
    update = spread(update, "branch", 0)
    pair_one = pairwise_state + update
    normed_one = layer_normalize(pair_one)
    start_rows = jnp.einsum("ijc,ch->hij", normed_one, starting_bias_weight, precision=highest)
    start_full, live_float = (
        lax.all_gather(start_rows, "res", axis=1, tiled=True),
        lax.all_gather(residue_present_mask.astype(jnp.float32), "res", axis=0, tiled=True),
    )
    live_keys = live_float > 0.5

    def starting():
        query_matrix = linear_project(normed_one, starting_projection_weight[0])
        key_matrix = linear_project(normed_one, starting_projection_weight[1])
        value_matrix = linear_project(normed_one, starting_projection_weight[2])
        gate_matrix = linear_project(normed_one, starting_projection_weight[3])

        def starting_one_row(operands):
            return attend(
                operands[0], operands[1], operands[2], operands[3], start_full, live_keys, HEADS_Z
            )

        gated_output = lax.map(
            starting_one_row, (query_matrix, key_matrix, value_matrix, gate_matrix)
        )
        return pair_one + linear_project(gated_output, starting_output_weight)

    pairwise_second = lax.cond(alignment_present_flag, lambda: jnp.zeros_like(pair_one), starting)
    normed_two = layer_normalize(pairwise_second)
    end_rows = jnp.einsum("ijc,ch->hij", normed_two, ending_bias_weight, precision=highest)
    end_full = lax.all_gather(end_rows, "res", axis=1, tiled=True)
    end_score = jnp.transpose(end_full, (0, 2, 1))
    normed_cols = lax.all_to_all(normed_two, "res", split_axis=1, concat_axis=0, tiled=True)
    column_shape = normed_cols.shape

    def ending():
        ending_q, ending_k, ending_v, ending_g = (
            linear_project(normed_cols, ending_projection_weight[0]),
            linear_project(normed_cols, ending_projection_weight[1]),
            linear_project(normed_cols, ending_projection_weight[2]),
            linear_project(normed_cols, ending_projection_weight[3]),
        )

        def one_column(column, buffer):
            result = attend(
                lax.dynamic_index_in_dim(ending_q, column, 1, keepdims=False),
                lax.dynamic_index_in_dim(ending_k, column, 1, keepdims=False),
                lax.dynamic_index_in_dim(ending_v, column, 1, keepdims=False),
                lax.dynamic_index_in_dim(ending_g, column, 1, keepdims=False),
                end_score,
                live_keys,
                HEADS_Z,
            )
            return lax.dynamic_update_index_in_dim(buffer, result, column, 1)

        gated_cols = lax.fori_loop(0, ending_q.shape[1], one_column, jnp.zeros_like(ending_q))
        return linear_project(gated_cols, ending_output_weight)

    ending_delta = lax.cond(
        alignment_present_flag, lambda: jnp.zeros(column_shape, jnp.float32), ending
    )
    pair_delta = lax.all_to_all(ending_delta, "res", split_axis=0, concat_axis=1, tiled=True)
    pairwise_result = pairwise_second + pair_delta
    sequence_halves = sequence_count // 2
    halved_width = pair_width // 2
    selected_alignment, selected_pairwise = partner(
        (alignment_result[sequence_halves:], pairwise_result[:, :, :halved_width]), "branch", 0
    )
    closing_alignment = jnp.where(
        alignment_present_flag, alignment_result[:sequence_halves], selected_alignment
    )
    final_pairwise = jnp.where(
        alignment_present_flag, selected_pairwise, pairwise_result[:, :, halved_width:]
    )
    return (closing_alignment, final_pairwise)


def solution(mesh):
    in_specs = (
        P(None, "res", None),
        P("res", None, None),
        P(None, "res"),
        P("res"),
        P(),
        P(),
        P(),
        P(),
        P(),
        P(),
        P(),
        P(),
        P(),
        P(),
        P(),
        P(),
    )
    out_specs = (P("branch", "res", None), P("res", None, "branch"))
    return jax.shard_map(
        per_device, mesh=mesh, in_specs=in_specs, out_specs=out_specs, check_vma=False
    )
```

profile of v0, /device:TPU:0, one launch (start us, length us, event | category | flops | bytes accessed | tf_op | source)
XLA Modules:
  0.0 355.1 jit_solution(5219426426211909906)
XLA Ops:
  8.8 1.8 fusion.82
  12.4 2.9 fusion.79
  16.0 7.4 %all-to-all-start.1 = ((f32[16,8,6]{1,2,0:T(8,128)}), f32[16,8,6]{1,2,0:T(8,128)}, u32[]{:S(2)}, u32[]{:S(2)}) async-start(f32[16,8,6]{1,2,0:T(8,128)} %copy.256), calls=%async_computation.1 | async-start | bytes 131072 | tf_op jit(solution)/shard_map/all_to_all | solution.py:117
  24.8 21.9 %all-gather = f32[16,6,128]{2,1,0:T(8,128)S(1)} all-gather(f32[1,6,128]{2,1,0:T(8,128)S(1)} %get-tuple-element.724), channel_id=1, replica_groups=mesh['branch'=2,'res'=16] {'res'}, dimensions={0}, use_global_device_ids=true | all-gather | bytes 52224 | tf_op jit(solution)/shard_map/all_gather | solution.py:150
  46.7 2.2 convolution_bitcast_fusion.4
  48.9 8.9 %all-gather.3.cloned.1.call-done = f32[96,32,128]{2,1,0:T(8,128)} async-done(((f32[6,32,128]{2,1,0:T(8,128)}), f32[96,32,128]{2,1,0:T(8,128)}) %all-gather.3.cloned.1.call-update) | async-done | bytes 1572880 | tf_op jit(solution)/shard_map/all_gather | solution.py:149
  57.8 35.2 %conditional.7 = (f32[6,96,128]{2,1,0:T(8,128)}) conditional(s32[]{:T(128)} %convert_element_type.6, () %tuple.72, (f32[6,128]{1,0:T(8,128)S(1)}, f32[6,32,128]{2,1,0:T(8,128)S(1)}, f32[96,32,128]{2,1,0:T(8,128)}, f32[1024,128]{1,0:T(8,128)S(1)}, f32[16,6,128]{2,1,0:T(8,128)S(1)}) %tuple.207), branch_computations={%region_13.14_spmd, %region_14.17_spmd} | conditional | flops 302174304 | bytes 7230381 | solution.py:152
  57.8 2.4 copy.264
  60.2 32.8 %while.40 = (s32[]{:T(128)}, f32[6,96,128]{2,1,0:T(8,128)}, f32[6,32,128]{2,1,0:T(8,128)S(1)}, f32[96,32,128]{2,0,1:T(8,128)S(1)}, f32[1024,128]{1,0:T(8,128)S(1...) while((s32[]{:T(128)}, f32[6,96,128]{2,1,0:T(8,128)}, f32[6,32,128]{2,1,0:T(8,128)S(1)}, ...), condition=%wide.region_16.16_spmd, body=%wide.region_15.15_spmd.sunk | while | flops 302149728 | bytes 3786589 | solution.py:72
  60.2 3.3 convolution_bitcast_fusion.8
  64.0 1.7 fusion.173
  65.7 3.3 convolution_bitcast_fusion.8
  69.5 1.7 fusion.173
  71.1 3.3 convolution_bitcast_fusion.8
  74.9 1.7 fusion.173
  76.6 3.3 convolution_bitcast_fusion.8
  80.4 1.7 fusion.173
  82.1 3.3 convolution_bitcast_fusion.8
  85.8 1.7 fusion.173
  87.5 3.3 convolution_bitcast_fusion.8
  91.3 1.7 fusion.173
  93.0 1.7 broadcast_select_fusion
  94.8 31.4 %all-reduce = f32[96]{0:T(128)S(1)} all-reduce(f32[96]{0:T(128)S(1)} %convert_dynamic-update-slice_fusion), channel_id=1, replica_groups=mesh['branch'=2,'res'=16] {'res'}, use_global_device_ids=true, to_apply=%add | all-reduce | flops 96 | bytes 768
  127.7 3.8 %all-to-all-start = ((f32[128,6,256]{2,1,0:T(8,128)}), f32[128,6,256]{2,1,0:T(8,128)S(1)}, u32[]{:S(2)}, u32[]{:S(2)}) async-start(f32[128,6,256]{2,1,0:T(8,128)} %fusion.80), calls=%async_computation | async-start | bytes 2097152 | tf_op jit(solution)/shard_map/all_to_all | solution.py:116
  132.4 33.2 %all_gather.22 = f32[4,96,96]{2,0,1:T(4,128)S(1)} all-gather(f32[4,6,96]{2,0,1:T(4,128)S(1)} %convolution_bitcast_fusion.6), channel_id=1, replica_groups=mesh['branch'=2,'res'=16] {'res'}, dimensions={1}, use_global_device_ids=true | all-gather | bytes 156672 | tf_op jit(solution)/shard_map/all_gather | solution.py:162
  167.3 5.9 %all-to-all-start.3 = ((f32[6,96,128]{2,0,1:T(8,128)}), f32[6,96,128]{2,0,1:T(8,128)}, u32[]{:S(2)}, u32[]{:S(2)}) async-start(f32[6,96,128]{2,0,1:T(8,128)} %fusion.85), calls=%async_computation.3 | async-start | bytes 786432 | tf_op jit(solution)/shard_map/all_to_all | solution.py:188
  173.2 33.9 %psum.14 = f32[8,6,96]{2,0,1:T(8,128)S(1)} all-reduce(f32[8,6,96]{2,0,1:T(8,128)S(1)} %broadcast_select_fusion.1), channel_id=1, replica_groups=mesh['branch'=2,'res'=16] {'branch'}, use_global_device_ids=true, to_apply=%region_6.7 | all-reduce | flops 4608 | bytes 36864 | tf_op jit(solution)/shard_map/psum | solution.py:16
  207.2 22.8 %all_gather.18 = f32[8,96,96]{2,0,1:T(8,128)S(1)} all-gather(f32[8,6,96]{2,0,1:T(8,128)S(1)} %psum.14), channel_id=1, replica_groups=mesh['branch'=2,'res'=16] {'res'}, dimensions={1}, use_global_device_ids=true | all-gather | bytes 313344 | tf_op jit(solution)/shard_map/all_gather | solution.py:114
  231.1 53.1 %conditional.6 = (f32[8,96,256]{2,1,0:T(8,128)S(1)}) conditional(s32[]{:T(128)} %convert_element_type.6, () %tuple.68, (f32[4,256,256]{2,1,0:T(8,128)}, f32[8,16,6,256]{3,0,1,2:T(8,128)}, f32[8,16,6]{0,2,1:T(8,128)}, f32[8,96,96]{2,0,1:T(8,128)S(1)}, f32[256,256]{1,0:T(8,128)}) %tuple.209), branch_computations={%region_7.8_spmd, %region_8.13_spmd} | conditional | flops 3077209344 | bytes 19131672 | solution.py:143
  233.9 2.3 fusion.14
  236.1 2.3 fusion.16
  238.4 2.3 fusion.18
  242.0 39.1 %while.39 = (s32[]{:T(128)}, f32[8,96,256]{1,2,0:T(8,128)}, f32[8,96,256]{1,2,0:T(8,128)}, f32[8,96,256]{1,2,0:T(8,128)}, pred[8,96]{1,0:T(8,128)(4,1)S(1)}, /*i...) while((s32[]{:T(128)}, f32[8,96,256]{1,2,0:T(8,128)}, ...), condition=%wide.region_12.12_spmd, body=%wide.region_9.11_spmd.sunk | while | flops 57309696 | bytes 2539401 | solution.py:138
  245.4 1.6 constant_dynamic-update-slice_fusion.8
  250.2 1.6 constant_dynamic-update-slice_fusion.8
  255.1 1.6 constant_dynamic-update-slice_fusion.8
  260.0 1.6 constant_dynamic-update-slice_fusion.8
  264.9 1.6 constant_dynamic-update-slice_fusion.8
  269.8 1.6 constant_dynamic-update-slice_fusion.8
  274.7 1.6 constant_dynamic-update-slice_fusion.8
  279.6 1.6 constant_dynamic-update-slice_fusion.8
  281.2 3.0 fusion.20
  285.6 3.7 %all-to-all-start.2 = ((f32[8,96,256]{2,0,1:T(8,128)}), f32[8,96,256]{2,0,1:T(8,128)S(1)}, u32[]{:S(2)}, u32[]{:S(2)}) async-start(f32[8,96,256]{2,0,1:T(8,128)} %copy.260), calls=%async_computation.2 | async-start | bytes 1572864 | tf_op jit(solution)/shard_map/all_to_all | solution.py:144
  289.4 1.6 convolution_bitcast_fusion.5
  291.0 28.1 %all_gather.23 = f32[4,96,96]{2,0,1:T(4,128)S(1)} all-gather(f32[4,6,96]{2,0,1:T(4,128)S(1)} %convolution_bitcast_fusion.5), channel_id=1, replica_groups=mesh['branch'=2,'res'=16] {'res'}, dimensions={1}, use_global_device_ids=true | all-gather | bytes 156672 | tf_op jit(solution)/shard_map/all_gather | solution.py:186
  321.5 4.5 %all-to-all-start.4 = ((f32[96,6,128]{2,1,0:T(8,128)}), f32[96,6,128]{2,1,0:T(8,128)S(1)}, u32[]{:S(2)}, u32[]{:S(2)}) async-start(f32[96,6,128]{2,1,0:T(8,128)} %copy.274), calls=%async_computation.4 | async-start | bytes 786432 | tf_op jit(solution)/shard_map/all_to_all | solution.py:217
  327.1 11.0 %all-to-all-done.4 = f32[96,6,128]{2,1,0:T(8,128)S(1)} async-done(((f32[96,6,128]{2,1,0:T(8,128)}), f32[96,6,128]{2,1,0:T(8,128)S(1)}, u32[]{:S(2)}, u32[]{:S(2)}) %all-to-all-start.4) | async-done | bytes 294944 | tf_op jit(solution)/shard_map/all_to_all | solution.py:217
  339.3 8.0 %collective-permute-done.1 = f32[6,96,64]{2,1,0:T(8,128)S(1)} collective-permute-done((f32[6,96,64]{2,1,0:T(8,128)S(1)}, f32[6,96,64]{2,1,0:T(8,128)S(1)}, u32[]{:S(2)}, u32[]{:S(2)}) %collective-permute-start.1) | collective-permute-done | bytes 147488 | tf_op jit(solution)/shard_map/ppermute | solution.py:26
  (165 shorter events, 49.8 us)
Async XLA Ops:
  7.2 5.2 %copy-start = (f32[256,32]{0,1:T(8,128)S(1)}, f32[256,32]{0,1:T(8,128)}, u32[]{:S(2)}) copy-start(f32[256,32]{0,1:T(8,128)} %param.42) | copy-start | bytes 98308
  7.2 3.6 %copy-start.2 = (f32[128,6,256]{2,0,1:T(8,128)S(1)}, f32[128,6,256]{2,0,1:T(8,128)}, u32[]{:S(2)}) copy-start(f32[128,6,256]{2,0,1:T(8,128)} %param.34) | copy-start | bytes 2359300
  7.2 50.6 %all-gather.3.cloned.1.call-start = ((), (), s32[]{:S(2)}) async-start(), calls=%async_computation.5 | async-start | bytes 1671168 | tf_op jit(solution)/shard_map/all_gather | solution.py:149
  8.6 3.7 %copy-start.12 = (s32[128,6]{0,1:T(8,128)S(1)}, s32[128,6]{0,1:T(8,128)}, u32[]{:S(2)}) copy-start(s32[128,6]{0,1:T(8,128)} %param.36) | copy-start | bytes 9220
  10.8 12.7 %copy-start.17 = (u32[32]{0:T(128)S(1)}, u32[32]{0:T(128)}, u32[]{:S(2)}) copy-start(u32[32]{0:T(128)} %constant.198) | copy-start | bytes 388
  10.8 35.9 %copy-start.11 = (f32[256,32]{0,1:T(8,128)S(1)}, f32[256,32]{0,1:T(8,128)}, u32[]{:S(2)}) copy-start(f32[256,32]{0,1:T(8,128)} %param.41) | copy-start | bytes 98308
  12.4 45.4 %copy-start.1 = (f32[1024,128]{1,0:T(8,128)S(1)}, f32[1024,128]{1,0:T(8,128)}, u32[]{:S(2)}) copy-start(f32[1024,128]{1,0:T(8,128)} %param.43) | copy-start | bytes 1572868
  16.0 111.7 %all-to-all-start.1 = ((f32[16,8,6]{1,2,0:T(8,128)}), f32[16,8,6]{1,2,0:T(8,128)}, u32[]{:S(2)}, u32[]{:S(2)}) async-start(f32[16,8,6]{1,2,0:T(8,128)} %copy.256), calls=%async_computation.1 | async-start | bytes 131072 | tf_op jit(solution)/shard_map/all_to_all | solution.py:117
  23.4 102.8 %all-reduce.3.cloned.1.call-start = ((), (), s32[]{:S(2)}) async-start(), calls=%async_computation.6 | async-start | bytes 589824 | tf_op jit(solution)/shard_map/psum | solution.py:16
  57.8 36.9 %copy-start.16 = (s32[6]{0:T(128)S(1)}, s32[6]{0:T(128)}, u32[]{:S(2)}) copy-start(s32[6]{0:T(128)} %param.37) | copy-start | bytes 76
  57.8 68.4 %copy-start.3 = (f32[6,96,128]{2,1,0:T(8,128)S(1)}, f32[6,96,128]{2,1,0:T(8,128)}, u32[]{:S(2)}) copy-start(f32[6,96,128]{2,1,0:T(8,128)} %param.35) | copy-start | bytes 884740
  127.4 4.4 %copy-start.14 = (f32[128,4]{0,1:T(4,128)S(1)}, f32[128,4]{0,1:T(4,128)}, u32[]{:S(2)}) copy-start(f32[128,4]{0,1:T(4,128)} %param.45) | copy-start | bytes 6148
  127.7 37.9 %copy-start.7 = (f32[4,128,128]{2,1,0:T(8,128)S(1)}, f32[4,128,128]{2,1,0:T(8,128)}, u32[]{:S(2)}) copy-start(f32[4,128,128]{2,1,0:T(8,128)} %param.44) | copy-start | bytes 786436
  127.7 37.9 %copy-start.9 = (f32[128,128]{1,0:T(8,128)S(1)}, f32[128,128]{1,0:T(8,128)}, u32[]{:S(2)}) copy-start(f32[128,128]{1,0:T(8,128)} %param.46) | copy-start | bytes 196612
  127.7 39.6 %all-to-all-start = ((f32[128,6,256]{2,1,0:T(8,128)}), f32[128,6,256]{2,1,0:T(8,128)S(1)}, u32[]{:S(2)}, u32[]{:S(2)}) async-start(f32[128,6,256]{2,1,0:T(8,128)} %fusion.80), calls=%async_computation | async-start | bytes 2097152 | tf_op jit(solution)/shard_map/all_to_all | solution.py:116
  165.6 7.6 %copy-start.13 = (f32[128,8]{0,1:T(8,128)S(1)}, f32[128,8]{0,1:T(8,128)}, u32[]{:S(2)}) copy-start(f32[128,8]{0,1:T(8,128)} %param.40) | copy-start | bytes 12292
  167.3 118.3 %all-to-all-start.3 = ((f32[6,96,128]{2,0,1:T(8,128)}), f32[6,96,128]{2,0,1:T(8,128)}, u32[]{:S(2)}, u32[]{:S(2)}) async-start(f32[6,96,128]{2,0,1:T(8,128)} %fusion.85), calls=%async_computation.3 | async-start | bytes 786432 | tf_op jit(solution)/shard_map/all_to_all | solution.py:188
  231.1 1.5 copy-start.6
  242.0 39.2 %copy-start.8 = (f32[256,256]{1,0:T(8,128)S(1)}, f32[256,256]{1,0:T(8,128)}, u32[]{:S(2)}) copy-start(f32[256,256]{1,0:T(8,128)} %get-tuple-element.359) | copy-start | bytes 786436 | tf_op jit(solution)/shard_map/cond
  284.2 5.1 %copy-start.15 = (f32[128,4]{0,1:T(4,128)S(1)}, f32[128,4]{0,1:T(4,128)}, u32[]{:S(2)}) copy-start(f32[128,4]{0,1:T(4,128)} %param.48) | copy-start | bytes 6148
  285.6 34.6 %copy-start.10 = (f32[128,128]{1,0:T(8,128)S(1)}, f32[128,128]{1,0:T(8,128)}, u32[]{:S(2)}) copy-start(f32[128,128]{1,0:T(8,128)} %param.49) | copy-start | bytes 196612
  285.6 35.9 %all-to-all-start.2 = ((f32[8,96,256]{2,0,1:T(8,128)}), f32[8,96,256]{2,0,1:T(8,128)S(1)}, u32[]{:S(2)}, u32[]{:S(2)}) async-start(f32[8,96,256]{2,0,1:T(8,128)} %copy.260), calls=%async_computation.2 | async-start | bytes 1572864 | tf_op jit(solution)/shard_map/all_to_all | solution.py:144
  321.5 16.6 %all-to-all-start.4 = ((f32[96,6,128]{2,1,0:T(8,128)}), f32[96,6,128]{2,1,0:T(8,128)S(1)}, u32[]{:S(2)}, u32[]{:S(2)}) async-start(f32[96,6,128]{2,1,0:T(8,128)} %copy.274), calls=%async_computation.4 | async-start | bytes 786432 | tf_op jit(solution)/shard_map/all_to_all | solution.py:217
  326.1 0.9 copy-start.4
  327.0 11.5 %copy-start.5 = (f32[128,6,256]{2,0,1:T(8,128)S(1)}, f32[128,6,256]{2,0,1:T(8,128)}, u32[]{:S(2)}) copy-start(f32[128,6,256]{2,0,1:T(8,128)} %copy-done.4) | copy-start | bytes 2359300
  327.0 11.5 %collective-permute-start = (f32[64,6,256]{2,0,1:T(8,128)S(1)}, f32[64,6,256]{2,0,1:T(8,128)S(1)}, u32[]{:S(2)}, u32[]{:S(2)}) collective-permute-start(f32[64,6,256]{2,0,1:T(8,128)S(1)} %slice.53), channel_id=1, source_target_pairs={{0,16},{16,0},{1,17},{17,1},{2,18},{18,2},{3,19},{19,3},{4,20},{20... | collective-permute-start | bytes 1179656 | tf_op jit(solution)/shard_map/ppermute | solution.py:26
  338.2 9.1 %collective-permute-start.1 = (f32[6,96,64]{2,1,0:T(8,128)S(1)}, f32[6,96,64]{2,1,0:T(8,128)S(1)}, u32[]{:S(2)}, u32[]{:S(2)}) collective-permute-start(f32[6,96,64]{2,1,0:T(8,128)S(1)} %bitcast.264), channel_id=1, source_target_pairs={{0,16},{16,0},{1,17},{17,1},{2,18},{18,2},{3,19},{19,3},{4,20},{20... | collective-permute-start | bytes 442376 | tf_op jit(solution)/shard_map/ppermute | solution.py:26
Sparse Core Ops, SparseCore 0:
  15.4 42.3 all-gather.2
  94.8 21.5 all-reduce.2
where the time goes:
time: 357 us; the launch traced here: 355 us
  blocking collectives  171 us (48%)
  matrix products  59.8 us (17%)
  local copies, waits for them, and re-layouts  30.1 us (8%)
  waiting for transfers between devices  28.2 us (8%)
  starting transfers between devices  25.5 us (7%)
  other arithmetic  24.2 us (7%)
  between operations  15.1 us (4%)
    psum x1, blocking collectives, spread(): return lax.psum(jnp.where(mine, value, jnp.zeros_like(value)), axis)  33.9 us
    all_gather x1, blocking collectives, per_device(): lax.all_gather(start_rows, 'res', axis=1, tiled=True)  33.2 us
    unnamed x1, blocking collectives  31.4 us
    all_gather x1, blocking collectives, per_device(): end_full = lax.all_gather(end_rows, 'res', axis=1, tiled=True)  28.1 us
    dot_general x13, matrix products, linear_project(): jnp.dot(values, weight, precision=highest, preferred_element_type=jnp.flo...  26.3 us
    all_gather x1, blocking collectives, per_device(): row_bias = lax.all_gather(own_rows, 'res', axis=1, tiled=True)  22.8 us
    all_gather x1, blocking collectives, per_device(): lax.all_gather(mask_rows, 'res', axis=0, tiled=True)  21.9 us
    dot_general x6, matrix products, outer_one_row(): jnp.einsum('cs,jes->jce', row_left, right_all, precision=highest)  19.8 us
  transfers between devices with their start and end apart: 9, of which 4 were waited for; matrix products, arithmetic and copies ran while one was open for 29% of the time, Pallas kernels for 0%

commit v1 on v0

--- a/solution.py
+++ b/solution.py
@@ -183,7 +183,7 @@
     pairwise_second = lax.cond(alignment_present_flag, lambda: jnp.zeros_like(pair_one), starting)
     normed_two = layer_normalize(pairwise_second)
     end_rows = jnp.einsum("ijc,ch->hij", normed_two, ending_bias_weight, precision=highest)
-    end_full = lax.all_gather(end_rows, "res", axis=1, tiled=True)
+    end_full = jnp.concatenate(lax.all_gather(end_rows, "res"), axis=1)
     end_score = jnp.transpose(end_full, (0, 2, 1))
     normed_cols = lax.all_to_all(normed_two, "res", split_axis=1, concat_axis=0, tiled=True)
     column_shape = normed_cols.shape

time: 357 us -> 350 us (0.980)
  blocking collectives: 171 us -> 167 us
    psum x1, blocking collectives: 33.9 us -> 26.7 us  [spread(): return lax.psum(jnp.where(mine, value, jnp.zeros_like(value)), axis)]
  transfers between devices with their start and end apart: 9 -> 9, of which waited for: 4 -> 3; matrix products, arithmetic and copies ran while one was open for 29% -> 29% of each run, Pallas kernels for 0% -> 0%
where the time goes in v1:
time: 350 us; the launch traced here: 348 us
  blocking collectives  167 us (48%)
  matrix products  60 us (17%)
  local copies, waits for them, and re-layouts  27.9 us (8%)
  waiting for transfers between devices  27.6 us (8%)
  starting transfers between devices  25.4 us (7%)
  other arithmetic  24.2 us (7%)
  between operations  15.1 us (4%)
    all_gather x1, blocking collectives, per_device(): lax.all_gather(start_rows, 'res', axis=1, tiled=True)  34.6 us
    unnamed x1, blocking collectives  31.4 us
    all_gather x1, blocking collectives, per_device(): end_full = jnp.concatenate(lax.all_gather(end_rows, 'res'), axis=1)  28.4 us
    psum x1, blocking collectives, spread(): return lax.psum(jnp.where(mine, value, jnp.zeros_like(value)), axis)  26.7 us
    dot_general x13, matrix products, linear_project(): jnp.dot(values, weight, precision=highest, preferred_element_type=jnp.flo...  26.4 us
    all_gather x1, blocking collectives, per_device(): lax.all_gather(mask_rows, 'res', axis=0, tiled=True)  23.4 us
    all_gather x1, blocking collectives, per_device(): row_bias = lax.all_gather(own_rows, 'res', axis=1, tiled=True)  22.9 us
    dot_general x6, matrix products, outer_one_row(): jnp.einsum('cs,jes->jce', row_left, right_all, precision=highest)  19.8 us
  transfers between devices with their start and end apart: 9, of which 3 were waited for; matrix products, arithmetic and copies ran while one was open for 29% of the time, Pallas kernels for 0%

profile of v1, /device:TPU:0, one launch (start us, length us, event | category | flops | bytes accessed | tf_op | source)
XLA Modules:
  0.0 348.4 jit_solution(8234035048731064037)
XLA Ops:
  8.8 1.8 fusion.82
  12.4 2.9 fusion.79
  16.0 7.4 %all-to-all-start.1 = ((f32[16,8,6]{1,2,0:T(8,128)}), f32[16,8,6]{1,2,0:T(8,128)}, u32[]{:S(2)}, u32[]{:S(2)}) async-start(f32[16,8,6]{1,2,0:T(8,128)} %copy.263), calls=%async_computation.1 | async-start | bytes 131072 | tf_op jit(solution)/shard_map/all_to_all | solution.py:117
  24.7 23.4 %all-gather.1 = f32[16,6,128]{2,1,0:T(8,128)} all-gather(f32[1,6,128]{2,1,0:T(8,128)S(1)} %get-tuple-element.719), channel_id=1, replica_groups=mesh['branch'=2,'res'=16] {'res'}, dimensions={0}, use_global_device_ids=true | all-gather | bytes 52224 | tf_op jit(solution)/shard_map/all_gather | solution.py:150
  48.2 2.2 convolution_bitcast_fusion.4
  50.4 7.4 %all-gather.4.cloned.1.call-done = f32[96,32,128]{2,1,0:T(8,128)} async-done(((f32[6,32,128]{2,1,0:T(8,128)}), f32[96,32,128]{2,1,0:T(8,128)}) %all-gather.4.cloned.1.call-update) | async-done | bytes 1572880 | tf_op jit(solution)/shard_map/all_gather | solution.py:149
  57.8 35.2 %conditional.7 = (f32[6,96,128]{2,1,0:T(8,128)}) conditional(s32[]{:T(128)} %convert_element_type.6, () %tuple.72, (f32[6,128]{1,0:T(8,128)S(1)}, f32[6,32,128]{2,1,0:T(8,128)S(1)}, f32[96,32,128]{2,1,0:T(8,128)}, f32[1024,128]{1,0:T(8,128)S(1)}, f32[16,6,128]{2,1,0:T(8,128)}) %tuple.206), branch_computations={%region_13.14_spmd, %region_14.17_spmd} | conditional | flops 302174304 | bytes 7427017 | solution.py:152
  57.8 2.4 copy.271
  60.2 32.8 %while.40 = (s32[]{:T(128)}, f32[6,96,128]{2,1,0:T(8,128)}, f32[6,32,128]{2,1,0:T(8,128)S(1)}, f32[96,32,128]{2,0,1:T(8,128)S(1)}, f32[1024,128]{1,0:T(8,128)S(1...) while((s32[]{:T(128)}, f32[6,96,128]{2,1,0:T(8,128)}, f32[6,32,128]{2,1,0:T(8,128)S(1)}, ...), condition=%wide.region_16.16_spmd, body=%wide.region_15.15_spmd.sunk | while | flops 302149728 | bytes 3786589 | solution.py:72
  60.3 3.3 convolution_bitcast_fusion.8
  64.0 1.7 fusion.173
  65.7 3.3 convolution_bitcast_fusion.8
  69.5 1.7 fusion.173
  71.2 3.3 convolution_bitcast_fusion.8
  75.0 1.7 fusion.173
  76.6 3.3 convolution_bitcast_fusion.8
  80.4 1.7 fusion.173
  82.1 3.3 convolution_bitcast_fusion.8
  85.9 1.7 fusion.173
  87.6 3.3 convolution_bitcast_fusion.8
  91.3 1.7 fusion.173
  93.0 1.7 broadcast_select_fusion
  94.9 31.4 %all-reduce = f32[96]{0:T(128)S(1)} all-reduce(f32[96]{0:T(128)S(1)} %convert_dynamic-update-slice_fusion), channel_id=1, replica_groups=mesh['branch'=2,'res'=16] {'res'}, use_global_device_ids=true, to_apply=%add | all-reduce | flops 96 | bytes 768
  127.7 3.7 %all-to-all-start = ((f32[128,6,256]{2,1,0:T(8,128)}), f32[128,6,256]{2,1,0:T(8,128)S(1)}, u32[]{:S(2)}, u32[]{:S(2)}) async-start(f32[128,6,256]{2,1,0:T(8,128)} %fusion.80), calls=%async_computation | async-start | bytes 2097152 | tf_op jit(solution)/shard_map/all_to_all | solution.py:116
  132.3 34.6 %all_gather.25 = f32[4,96,96]{2,0,1:T(4,128)} all-gather(f32[4,6,96]{2,0,1:T(4,128)S(1)} %convolution_bitcast_fusion.6), channel_id=1, replica_groups=mesh['branch'=2,'res'=16] {'res'}, dimensions={1}, use_global_device_ids=true | all-gather | bytes 156672 | tf_op jit(solution)/shard_map/all_gather | solution.py:162
  168.6 5.8 %all-to-all-start.3 = ((f32[6,96,128]{2,0,1:T(8,128)}), f32[6,96,128]{2,0,1:T(8,128)S(1)}, u32[]{:S(2)}, u32[]{:S(2)}) async-start(f32[6,96,128]{2,0,1:T(8,128)} %fusion.85), calls=%async_computation.3 | async-start | bytes 786432 | tf_op jit(solution)/shard_map/all_to_all | solution.py:188
  174.4 26.7 %psum.14 = f32[8,6,96]{2,0,1:T(8,128)S(1)} all-reduce(f32[8,6,96]{2,0,1:T(8,128)S(1)} %broadcast_select_fusion.1), channel_id=1, replica_groups=mesh['branch'=2,'res'=16] {'branch'}, use_global_device_ids=true, to_apply=%region_6.7 | all-reduce | flops 4608 | bytes 36864 | tf_op jit(solution)/shard_map/psum | solution.py:16
  201.2 22.9 %all_gather.21 = f32[8,96,96]{2,0,1:T(8,128)S(1)} all-gather(f32[8,6,96]{2,0,1:T(8,128)S(1)} %psum.14), channel_id=1, replica_groups=mesh['branch'=2,'res'=16] {'res'}, dimensions={1}, use_global_device_ids=true | all-gather | bytes 313344 | tf_op jit(solution)/shard_map/all_gather | solution.py:114
  224.3 53.2 %conditional.6 = (f32[8,96,256]{2,1,0:T(8,128)S(1)}) conditional(s32[]{:T(128)} %convert_element_type.6, () %tuple.68, (f32[4,256,256]{2,1,0:T(8,128)}, f32[8,16,6,256]{3,0,1,2:T(8,128)S(1)}, f32[8,16,6]{0,2,1:T(8,128)}, f32[8,96,96]{2,0,1:T(8,128)S(1)}, f32[256,256]{1,0:T(8,128)}) %tuple.208), branch_computations={%region_7.8_spmd, %region_8.13_spmd} | conditional | flops 3077209344 | bytes 19131672 | solution.py:143
  227.1 2.3 fusion.14
  229.4 2.3 fusion.16
  231.7 2.3 fusion.18
  235.4 39.1 %while.39 = (s32[]{:T(128)}, f32[8,96,256]{1,2,0:T(8,128)}, f32[8,96,256]{1,2,0:T(8,128)}, f32[8,96,256]{1,2,0:T(8,128)}, pred[8,96]{1,0:T(8,128)(4,1)S(1)}, /*i...) while((s32[]{:T(128)}, f32[8,96,256]{1,2,0:T(8,128)}, ...), condition=%wide.region_12.12_spmd, body=%wide.region_9.11_spmd.sunk | while | flops 57309696 | bytes 2539401 | solution.py:138
  238.7 1.6 constant_dynamic-update-slice_fusion.8
  243.6 1.6 constant_dynamic-update-slice_fusion.8
  248.5 1.6 constant_dynamic-update-slice_fusion.8
  253.3 1.6 constant_dynamic-update-slice_fusion.8
  258.2 1.6 constant_dynamic-update-slice_fusion.8
  263.1 1.6 constant_dynamic-update-slice_fusion.8
  268.0 1.6 constant_dynamic-update-slice_fusion.8
  272.9 1.6 constant_dynamic-update-slice_fusion.8
  274.5 3.0 fusion.20
  278.9 3.7 %all-to-all-start.2 = ((f32[8,96,256]{2,0,1:T(8,128)}), f32[8,96,256]{2,0,1:T(8,128)S(1)}, u32[]{:S(2)}, u32[]{:S(2)}) async-start(f32[8,96,256]{2,0,1:T(8,128)} %copy.267), calls=%async_computation.2 | async-start | bytes 1572864 | tf_op jit(solution)/shard_map/all_to_all | solution.py:144
  282.7 1.6 convolution_bitcast_fusion.5
  284.3 28.4 %all-gather = f32[64,6,96]{2,1,0:T(8,128)S(1)} all-gather(f32[4,6,96]{2,1,0:T(8,128)S(1)} %copy.279), channel_id=2, replica_groups=mesh['branch'=2,'res'=16] {'res'}, dimensions={0}, use_global_device_ids=true | all-gather | bytes 156672 | tf_op jit(solution)/shard_map/all_gather | solution.py:186
  314.8 4.5 %all-to-all-start.4 = ((f32[96,6,128]{2,1,0:T(8,128)}), f32[96,6,128]{2,1,0:T(8,128)S(1)}, u32[]{:S(2)}, u32[]{:S(2)}) async-start(f32[96,6,128]{2,1,0:T(8,128)} %copy.283), calls=%async_computation.4 | async-start | bytes 786432 | tf_op jit(solution)/shard_map/all_to_all | solution.py:217
  319.5 11.9 %all-to-all-done.4 = f32[96,6,128]{2,1,0:T(8,128)S(1)} async-done(((f32[96,6,128]{2,1,0:T(8,128)}), f32[96,6,128]{2,1,0:T(8,128)S(1)}, u32[]{:S(2)}, u32[]{:S(2)}) %all-to-all-start.4) | async-done | bytes 294944 | tf_op jit(solution)/shard_map/all_to_all | solution.py:217
  332.4 8.2 %collective-permute-done.1 = f32[6,96,64]{2,1,0:T(8,128)S(1)} collective-permute-done((f32[6,96,64]{2,1,0:T(8,128)S(1)}, f32[6,96,64]{2,1,0:T(8,128)S(1)}, u32[]{:S(2)}, u32[]{:S(2)}) %collective-permute-start.1) | collective-permute-done | bytes 147488 | tf_op jit(solution)/shard_map/ppermute | solution.py:26
  (161 shorter events, 47.4 us)
Async XLA Ops:
  7.2 5.2 %copy-start = (f32[256,32]{0,1:T(8,128)S(1)}, f32[256,32]{0,1:T(8,128)}, u32[]{:S(2)}) copy-start(f32[256,32]{0,1:T(8,128)} %param.42) | copy-start | bytes 98308
  7.2 3.6 %copy-start.2 = (f32[128,6,256]{2,0,1:T(8,128)S(1)}, f32[128,6,256]{2,0,1:T(8,128)}, u32[]{:S(2)}) copy-start(f32[128,6,256]{2,0,1:T(8,128)} %param.34) | copy-start | bytes 2359300
  7.2 50.6 %all-gather.4.cloned.1.call-start = ((), (), s32[]{:S(2)}) async-start(), calls=%async_computation.5 | async-start | bytes 1671168 | tf_op jit(solution)/shard_map/all_gather | solution.py:149
  8.6 3.7 %copy-start.9 = (s32[128,6]{0,1:T(8,128)S(1)}, s32[128,6]{0,1:T(8,128)}, u32[]{:S(2)}) copy-start(s32[128,6]{0,1:T(8,128)} %param.36) | copy-start | bytes 9220
  10.8 12.7 %copy-start.14 = (u32[32]{0:T(128)S(1)}, u32[32]{0:T(128)}, u32[]{:S(2)}) copy-start(u32[32]{0:T(128)} %constant.198) | copy-start | bytes 388
  10.8 37.4 %copy-start.8 = (f32[256,32]{0,1:T(8,128)S(1)}, f32[256,32]{0,1:T(8,128)}, u32[]{:S(2)}) copy-start(f32[256,32]{0,1:T(8,128)} %param.41) | copy-start | bytes 98308
  12.4 45.4 %copy-start.1 = (f32[1024,128]{1,0:T(8,128)S(1)}, f32[1024,128]{1,0:T(8,128)}, u32[]{:S(2)}) copy-start(f32[1024,128]{1,0:T(8,128)} %param.43) | copy-start | bytes 1572868
  16.0 111.7 %all-to-all-start.1 = ((f32[16,8,6]{1,2,0:T(8,128)}), f32[16,8,6]{1,2,0:T(8,128)}, u32[]{:S(2)}, u32[]{:S(2)}) async-start(f32[16,8,6]{1,2,0:T(8,128)} %copy.263), calls=%async_computation.1 | async-start | bytes 131072 | tf_op jit(solution)/shard_map/all_to_all | solution.py:117
  23.4 102.8 %all-reduce.3.cloned.1.call-start = ((), (), s32[]{:S(2)}) async-start(), calls=%async_computation.6 | async-start | bytes 589824 | tf_op jit(solution)/shard_map/psum | solution.py:16
  57.8 37.0 %copy-start.13 = (s32[6]{0:T(128)S(1)}, s32[6]{0:T(128)}, u32[]{:S(2)}) copy-start(s32[6]{0:T(128)} %param.37) | copy-start | bytes 76
  57.8 68.4 %copy-start.3 = (f32[6,96,128]{2,1,0:T(8,128)S(1)}, f32[6,96,128]{2,1,0:T(8,128)}, u32[]{:S(2)}) copy-start(f32[6,96,128]{2,1,0:T(8,128)} %param.35) | copy-start | bytes 884740
  57.8 2.4 copy-start.5
  127.4 4.2 %copy-start.11 = (f32[128,4]{0,1:T(4,128)S(1)}, f32[128,4]{0,1:T(4,128)}, u32[]{:S(2)}) copy-start(f32[128,4]{0,1:T(4,128)} %param.45) | copy-start | bytes 6148
  127.7 40.8 %all-to-all-start = ((f32[128,6,256]{2,1,0:T(8,128)}), f32[128,6,256]{2,1,0:T(8,128)S(1)}, u32[]{:S(2)}, u32[]{:S(2)}) async-start(f32[128,6,256]{2,1,0:T(8,128)} %fusion.80), calls=%async_computation | async-start | bytes 2097152 | tf_op jit(solution)/shard_map/all_to_all | solution.py:116
  166.9 7.5 %copy-start.10 = (f32[128,8]{0,1:T(8,128)S(1)}, f32[128,8]{0,1:T(8,128)}, u32[]{:S(2)}) copy-start(f32[128,8]{0,1:T(8,128)} %param.40) | copy-start | bytes 12292
  168.6 110.3 %all-to-all-start.3 = ((f32[6,96,128]{2,0,1:T(8,128)}), f32[6,96,128]{2,0,1:T(8,128)S(1)}, u32[]{:S(2)}, u32[]{:S(2)}) async-start(f32[6,96,128]{2,0,1:T(8,128)} %fusion.85), calls=%async_computation.3 | async-start | bytes 786432 | tf_op jit(solution)/shard_map/all_to_all | solution.py:188
  224.5 1.2 copy-start.4
  235.3 39.1 %copy-start.6 = (f32[256,256]{1,0:T(8,128)S(1)}, f32[256,256]{1,0:T(8,128)}, u32[]{:S(2)}) copy-start(f32[256,256]{1,0:T(8,128)} %get-tuple-element.359) | copy-start | bytes 786436 | tf_op jit(solution)/shard_map/cond
  277.5 5.1 %copy-start.12 = (f32[128,4]{0,1:T(4,128)S(1)}, f32[128,4]{0,1:T(4,128)}, u32[]{:S(2)}) copy-start(f32[128,4]{0,1:T(4,128)} %param.48) | copy-start | bytes 6148
  278.9 34.6 %copy-start.7 = (f32[128,128]{1,0:T(8,128)S(1)}, f32[128,128]{1,0:T(8,128)}, u32[]{:S(2)}) copy-start(f32[128,128]{1,0:T(8,128)} %param.49) | copy-start | bytes 196612
  278.9 35.9 %all-to-all-start.2 = ((f32[8,96,256]{2,0,1:T(8,128)}), f32[8,96,256]{2,0,1:T(8,128)S(1)}, u32[]{:S(2)}, u32[]{:S(2)}) async-start(f32[8,96,256]{2,0,1:T(8,128)} %copy.267), calls=%async_computation.2 | async-start | bytes 1572864 | tf_op jit(solution)/shard_map/all_to_all | solution.py:144
  314.8 16.6 %all-to-all-start.4 = ((f32[96,6,128]{2,1,0:T(8,128)}), f32[96,6,128]{2,1,0:T(8,128)S(1)}, u32[]{:S(2)}, u32[]{:S(2)}) async-start(f32[96,6,128]{2,1,0:T(8,128)} %copy.283), calls=%async_computation.4 | async-start | bytes 786432 | tf_op jit(solution)/shard_map/all_to_all | solution.py:217
  319.4 12.2 %collective-permute-start = (f32[64,6,256]{2,0,1:T(8,128)S(1)}, f32[64,6,256]{2,0,1:T(8,128)S(1)}, u32[]{:S(2)}, u32[]{:S(2)}) collective-permute-start(f32[64,6,256]{2,0,1:T(8,128)S(1)} %slice.53), channel_id=1, source_target_pairs={{0,16},{16,0},{1,17},{17,1},{2,18},{18,2},{3,19},{19,3},{4,20},{20... | collective-permute-start | bytes 1179656 | tf_op jit(solution)/shard_map/ppermute | solution.py:26
  331.5 9.1 %collective-permute-start.1 = (f32[6,96,64]{2,1,0:T(8,128)S(1)}, f32[6,96,64]{2,1,0:T(8,128)S(1)}, u32[]{:S(2)}, u32[]{:S(2)}) collective-permute-start(f32[6,96,64]{2,1,0:T(8,128)S(1)} %bitcast.270), channel_id=1, source_target_pairs={{0,16},{16,0},{1,17},{17,1},{2,18},{18,2},{3,19},{19,3},{4,20},{20... | collective-permute-start | bytes 442376 | tf_op jit(solution)/shard_map/ppermute | solution.py:26
Sparse Core Ops, SparseCore 0:
  15.4 42.3 all-gather.3
  94.9 21.5 all-reduce.2
